TPU v7x, 32 devices: a whole 2x2x4 slice. The times are simulated.
32 devices in a mesh: groups: 2 (over y), span: 4 (over x, core), head: 4 (over z).
Axes of the slice: x: 2, y: 2, z: 4, core: 2. Of those that a mesh axis runs over, the one named last changes fastest.
Arguments:
- queries: bfloat16 [4096, 1024], P(('groups', 'span', 'head')), parts along dimension 0, may hold values from -8 to 8
- keys: bfloat16 [4096, 1024], P(('groups', 'span', 'head')), parts along dimension 0, may hold values from -8 to 8
- values: bfloat16 [4096, 1024], P(('groups', 'span', 'head')), parts along dimension 0, may hold values from -6 to 6
- tile_offsets: int32 [32, 7], P(('groups', 'span')), parts along dimension 0, may hold values from 0 to 6, as said below
- timesteps: int32 [8], P(('groups', 'span')), parts along dimension 0, may hold values from 0 to 999
- time_weight: bfloat16 [256, 1024], P(None, 'head'), may hold values from -0.375 to 0.375
Outputs:
- attended: bfloat16 [4096, 1024], P(('groups', 'span', 'head')), parts along dimension 0
There are 2 independent parts, one for each index of `groups`. A program takes and returns all parts, laid end to end along the dimension named above; an argument that names none is the same for every part. Nothing has to cross between parts.
Inputs may be any that keep to these rules, and one draw needn't show every extreme that they name: `tile_offsets`: the first entry of each row is 0 and the 7 entries of a row are distinct.
All inputs are finite; a program needn't handle non-finite values.
Results may differ from a plain program's by a relative error of at most 0.0035.
Values may be sent and summed in bfloat16 or wider, within the bound.
No kernel may reach another device: no remote copies, remote signals or barrier semaphores. Data moves between devices by JAX's collectives and lax.ppermute only.
A program may use at most 64 MiB of HBM per device.

v0:
```python
import math
import jax
import jax.numpy as jnp
from jax import lax
from jax.sharding import PartitionSpec as P

HEAD_SIZE = 128
TILE = 128
FREQ = 256


def shifted(value, axis, by):
    size = lax.axis_size(axis)
    pairs = [(i, i + by) for i in range(size) if 0 <= i + by < size]
    return lax.ppermute(value, axis, pairs)


def local(queries, keys, values, tile_offsets, timesteps, time_weight):
    query_heads, key_heads, value_heads = (
        lax.all_to_all(queries, "head", split_axis=1, concat_axis=0, tiled=True),
        lax.all_to_all(keys, "head", split_axis=1, concat_axis=0, tiled=True),
        lax.all_to_all(values, "head", split_axis=1, concat_axis=0, tiled=True),
    )
    span_rows = query_heads.shape[0]
    width = query_heads.shape[1]
    heads_here = width // HEAD_SIZE
    tiles_here = span_rows // TILE
    reach = 3 * tiles_here // 2
    listed = tile_offsets.shape[1]
    tail_rows = (reach - tiles_here) * TILE
    resident = jnp.concatenate([key_heads, value_heads], axis=1)
    nearer = shifted(resident, "span", 1)
    farther = shifted(resident[span_rows - tail_rows :], "span", 2)
    window = jnp.concatenate([farther, nearer, resident], axis=0)
    window = window.reshape(reach + tiles_here, TILE, 2 * width)
    half = FREQ // 2
    freqs = jnp.exp(-math.log(10000.0) * jnp.arange(half, dtype=jnp.float32) / half)
    angles = timesteps.astype(jnp.float32)[:, None] * freqs[None, :]
    embedded = jnp.concatenate([jnp.cos(angles), jnp.sin(angles)], axis=1)
    gate = jnp.dot(embedded, time_weight.astype(jnp.float32), precision=lax.Precision.HIGHEST)
    gate_rows = gate.reshape(1, 1, heads_here, HEAD_SIZE)
    position = lax.axis_index("span")
    scale = HEAD_SIZE ** (-0.5)
    query_blocks = query_heads.reshape(tiles_here // 4, 4, TILE, heads_here, HEAD_SIZE)
    offset_blocks = tile_offsets.reshape(tiles_here // 4, 4, listed)

    def one_block(inputs):
        block, query_part, offsets = inputs
        local_tiles = block * 4 + jnp.arange(4, dtype=jnp.int32)
        source = local_tiles[:, None] - offsets
        usable = position * tiles_here + source >= 0
        picked = window[source + reach].reshape(4, listed * TILE, 2 * width)
        key_part = picked[:, :, :width].reshape(4, listed * TILE, heads_here, HEAD_SIZE)
        value_part = picked[:, :, width:].reshape(4, listed * TILE, heads_here, HEAD_SIZE)
        scores = (
            jnp.einsum("qthd,qkhd->qhtk", query_part, key_part, preferred_element_type=jnp.float32)
            * scale
        )
        keep = jnp.repeat(usable, TILE, axis=1)
        scores = jnp.where(keep[:, None, None, :], scores, -1e30)
        top = jnp.max(scores, axis=-1, keepdims=True)
        weights = jnp.exp(scores - top)
        total = jnp.sum(weights, axis=-1, keepdims=True)
        rounded = weights.astype(jnp.bfloat16)
        mixed = jnp.einsum(
            "qhtk,qkhd->qthd", rounded, value_part, preferred_element_type=jnp.float32
        )
        mixed = mixed / jnp.transpose(total, (0, 2, 1, 3))
        return (mixed * (1.0 + gate_rows)).astype(jnp.bfloat16)

    blocks = jnp.arange(tiles_here // 4, dtype=jnp.int32)
    gated = lax.map(one_block, (blocks, query_blocks, offset_blocks)).reshape(span_rows, width)
    return lax.all_to_all(gated, "head", split_axis=0, concat_axis=1, tiled=True)


def solution(mesh):
    return jax.shard_map(
        local,
        mesh=mesh,
        in_specs=(
            P(("groups", "span", "head"), None),
            P(("groups", "span", "head"), None),
            P(("groups", "span", "head"), None),
            P(("groups", "span"), None),
            P(("groups", "span")),
            P(None, "head"),
        ),
        out_specs=P(("groups", "span", "head"), None),
        check_vma=False,
    )
```

profile of v0, /device:TPU:7, one launch (start us, length us, event | category | flops | bytes accessed | tf_op | source)
XLA Modules:
  0.0 76.2 jit_solution(9081810094877849396)
XLA Ops:
  0.0 0.0 copy-start
  0.0 0.0 copy-start.2
  0.0 1.8 %copy.18 = bf16[128,1024]{0,1:T(8,128)(2,1)} copy(bf16[128,1024]{1,0:T(8,128)(2,1)} %param.8) | data formatting | bytes 524288 | tf_op args[2]
  1.8 4.6 %all-to-all-start.1 = ((bf16[128,4,256]{0,2,1:T(8,128)(2,1)}), bf16[128,4,256]{0,2,1:T(8,128)(2,1)S(1)}, u32[]{:S(2)}, u32[]{:S(2)}) async-start(bf16[128,4,256]{0,2,1:T(8,128)(2,1)} %bitcast.3), calls=%async_computation.1 | async-start | bytes 524288 | tf_op jit(solution)/shard_map/all_to_all | solution.py:22
  6.4 1.8 %copy.16 = bf16[128,1024]{0,1:T(8,128)(2,1)} copy(bf16[128,1024]{1,0:T(8,128)(2,1)} %param.7) | data formatting | bytes 524288 | tf_op args[1]
  8.2 0.7 add_compare_fusion
  8.9 5.1 %all-to-all-done.1 = bf16[128,4,256]{0,2,1:T(8,128)(2,1)S(1)} async-done(((bf16[128,4,256]{0,2,1:T(8,128)(2,1)}), bf16[128,4,256]{0,2,1:T(8,128)(2,1)S(1)}, u32[]{:S(2)}, u32[]{:S(2)}) %all-to-all-start.1) | async-done | bytes 262176 | tf_op jit(solution)/shard_map/all_to_all | solution.py:22
  14.0 3.4 %all-to-all-start = ((bf16[128,4,256]{0,2,1:T(8,128)(2,1)}), bf16[128,4,256]{0,2,1:T(8,128)(2,1)S(1)}, u32[]{:S(2)}, u32[]{:S(2)}) async-start(bf16[128,4,256]{0,2,1:T(8,128)(2,1)} %bitcast), calls=%async_computation | async-start | bytes 524288 | tf_op jit(solution)/shard_map/all_to_all | solution.py:21
  17.4 0.1 broadcast_bitcast_fusion
  17.5 1.8 %copy.22 = bf16[128,1024]{0,1:T(8,128)(2,1)} copy(bf16[128,1024]{1,0:T(8,128)(2,1)} %param.6) | data formatting | bytes 524288 | tf_op args[0]
  19.9 0.1 fusion.27
  20.0 0.0 copy-done
  20.0 0.1 fusion.22
  20.1 0.2 copy.19
  20.3 2.7 %all-to-all-done = bf16[128,4,256]{0,2,1:T(8,128)(2,1)S(1)} async-done(((bf16[128,4,256]{0,2,1:T(8,128)(2,1)}), bf16[128,4,256]{0,2,1:T(8,128)(2,1)S(1)}, u32[]{:S(2)}, u32[]{:S(2)}) %all-to-all-start) | async-done | bytes 262176 | tf_op jit(solution)/shard_map/all_to_all | solution.py:21
  23.0 3.4 %all-to-all-start.2 = ((bf16[128,4,256]{0,2,1:T(8,128)(2,1)}), bf16[128,4,256]{0,2,1:T(8,128)(2,1)S(1)}, u32[]{:S(2)}, u32[]{:S(2)}) async-start(bf16[128,4,256]{0,2,1:T(8,128)(2,1)} %bitcast.10), calls=%async_computation.2 | async-start | bytes 524288 | tf_op jit(solution)/shard_map/all_to_all | solution.py:20
  26.4 0.1 copy.17
  26.6 1.3 %collective-permute-start.1 = (bf16[512,512]{1,0:T(8,128)(2,1)S(1)}, bf16[512,512]{1,0:T(8,128)(2,1)S(1)}, u32[]{:S(2)}, u32[]{:S(2)}) collective-permute-start(bf16[512,512]{1,0:T(8,128)(2,1)S(1)} %pad_maximum_fusion), channel_id=1, source_target_pairs={{0,4},{4,8},{8,12},{1,5},{5,9},{9,13},{2,6},{6,10},{10,14},{3,7},{... | collective-permute-start | bytes 1572872 | tf_op jit(solution)/shard_map/ppermute | solution.py:15
  27.9 0.0 copy-done.2
  27.9 0.1 reshape.97
  28.1 1.3 %collective-permute-start = (bf16[256,512]{1,0:T(8,128)(2,1)S(1)}, bf16[256,512]{1,0:T(8,128)(2,1)S(1)}, u32[]{:S(2)}, u32[]{:S(2)}) collective-permute-start(bf16[256,512]{1,0:T(8,128)(2,1)S(1)} %fusion.21), channel_id=1, source_target_pairs={{0,8},{4,12},{1,9},{5,13},{2,10},{6,14},{3,11},{7,15},{16,24},{20,... | collective-permute-start | bytes 786440 | tf_op jit(solution)/shard_map/ppermute | solution.py:15
  29.4 16.3 %collective-permute-done = bf16[256,512]{1,0:T(8,128)(2,1)S(1)} collective-permute-done((bf16[256,512]{1,0:T(8,128)(2,1)S(1)}, bf16[256,512]{1,0:T(8,128)(2,1)S(1)}, u32[]{:S(2)}, u32[]{:S(2)}) %collective-permute-start) | collective-permute-done | bytes 262176 | tf_op jit(solution)/shard_map/ppermute | solution.py:15
  45.7 0.0 collective-permute-done.1
  45.7 0.1 maximum_maximum_fusion
  45.8 2.6 %gather_fusion = bf16[28,128,512]{2,1,0:T(8,128)(2,1)} fusion(bf16[10,128,512]{2,1,0:T(8,128)(2,1)S(1)} %bitcast.73, s32[1024]{0:T(1024)S(1)} %pad_clamp_fusion), kind=kCustom, calls=%fused_computation | custom fusion | bytes 7340144 | tf_op jit(solution)/shard_map/while/body/eval_jaxpr/gather | solution.py:52
  48.5 3.6 %fusion.32 = (bf16[4,896,256]{2,1,0:T(8,128)(2,1)S(1)}, bf16[4,896,256]{2,1,0:T(8,128)(2,1)}) fusion(bf16[4,896,512]{2,1,0:T(8,128)(2,1)} %bitcast.74), kind=kLoop, calls=%fused_computation.40 | loop fusion | bytes 7340032 | tf_op jit(solution)/shard_map/while/body/eval_jaxpr/slice | solution.py:53
  52.0 3.6 %copy.20 = bf16[4,896,256]{1,2,0:T(8,128)(2,1)} copy(bf16[4,896,256]{2,1,0:T(8,128)(2,1)} %get-tuple-element.18) | data formatting | bytes 3670016 | tf_op jit(solution)/shard_map/while/body/eval_jaxpr/slice | solution.py:54
  55.6 2.4 %copy.21 = bf16[4,896,256]{1,2,0:T(8,128)(2,1)} copy(bf16[4,896,256]{2,1,0:T(8,128)(2,1)S(1)} %get-tuple-element.17) | data formatting | bytes 3670016 | tf_op jit(solution)/shard_map/while/body/eval_jaxpr/slice | solution.py:53
  58.0 0.0 all-to-all-done.2
  58.0 0.0 copy-start.1
  58.0 2.6 %bitcast_reduce_fusion = (f32[4,2,128]{2,1,0:T(2,128)S(1)}, f32[4,2,896,128]{3,2,1,0:T(8,128)S(1)}) fusion(pred[4,896]{1,0:T(4,128)(4,1)S(1)} %bitcast.88, bf16[4,896,2,128]{1,3,2,0:T(8,128)(2,1)} %bitcast.75, bf16[4,128,2,128]{1,3,2,0:T(8,128)(2,1)S(1)} %bitcast.86), kind=kOutput, calls=%fused_computation.2 | convolution fusion | flops 237632512 | bytes 5774848 | tf_op jit(solution)/shard_map/while/body/eval_jaxpr/qthd,qkhd->qhtk/dot_general | solution.py:56
  60.6 1.1 %fusion.1 = f32[4,2,128]{2,1,0:T(2,128)S(1)} fusion(f32[4,2,896,128]{3,2,1,0:T(8,128)S(1)} %get-tuple-element.20, f32[4,2,128]{2,1,0:T(2,128)S(1)} %get-tuple-element.19, pred[4,896]{1,0:T(4,128)(4,1)S(1)} %bitcast.89), kind=kLoop, calls=%fused_computation.5 | loop fusion | flops 3668992 | bytes 3681792 | tf_op jit(solution)/shard_map/while/body/eval_jaxpr/reduce_sum | solution.py:63
  61.7 0.0 copy-done.1
  61.7 1.3 %fusion.18 = bf16[4,128,2,128]{1,3,2,0:T(8,128)(2,1)S(1)} fusion(bf16[4,896,2,128]{1,3,2,0:T(8,128)(2,1)S(1)} %bitcast.82, f32[4,2,896,128]{3,2,1,0:T(8,128)S(1)} %get-tuple-element.20, f32[4,2,128]{2,1,0:T(2,128)S(1)} %get-tuple-element.19, pred[4,896]{1,0:T(4,128)(4,1)S(1)} %bitcast.90, f32[2,128]{1,0:T(2,128)S(1)} %broadcast_add_fusion, ...), kind=kOutput, calls=%fused_computation.16 | convolution fusion | flops 238944256 | bytes 5779968 | tf_op jit(solution)/shard_map/while/body/eval_jaxpr/qhtk,qkhd->qthd/dot_general | solution.py:65
  63.0 12.3 %all_to_all.73 = bf16[4,128,256]{1,2,0:T(8,128)(2,1)S(1)} all-to-all(bf16[4,128,256]{1,2,0:T(8,128)(2,1)S(1)} %bitcast.87), channel_id=1, replica_groups=mesh['groups'=2,'span'=4,'head'=4] {'head'}, dimensions={0} | all-to-all | bytes 524288 | tf_op jit(solution)/shard_map/all_to_all | solution.py:73
  75.4 0.8 %copy.32 = bf16[128,1024]{1,0:T(8,128)(2,1)} copy(bf16[128,1024]{0,1:T(8,128)(2,1)S(1)} %bitcast.85) | data formatting | bytes 524288 | tf_op jit(solution)/shard_map/all_to_all | solution.py:73
  (6 shorter events, 0.1 us)
Async XLA Ops:
  0.0 20.0 %copy-start = (bf16[256,256]{1,0:T(8,128)(2,1)S(1)}, bf16[256,256]{1,0:T(8,128)(2,1)}, u32[]{:S(2)}) copy-start(bf16[256,256]{1,0:T(8,128)(2,1)} %param.11) | copy-start | bytes 393220
  0.0 27.9 %copy-start.2 = (s32[4,7]{1,0:T(4,128)S(1)}, s32[4,7]{1,0:T(4,128)}, u32[]{:S(2)}) copy-start(s32[4,7]{1,0:T(4,128)} %param.9) | copy-start | bytes 340
  1.8 12.2 %all-to-all-start.1 = ((bf16[128,4,256]{0,2,1:T(8,128)(2,1)}), bf16[128,4,256]{0,2,1:T(8,128)(2,1)S(1)}, u32[]{:S(2)}, u32[]{:S(2)}) async-start(bf16[128,4,256]{0,2,1:T(8,128)(2,1)} %bitcast.3), calls=%async_computation.1 | async-start | bytes 524288 | tf_op jit(solution)/shard_map/all_to_all | solution.py:22
  14.0 9.0 %all-to-all-start = ((bf16[128,4,256]{0,2,1:T(8,128)(2,1)}), bf16[128,4,256]{0,2,1:T(8,128)(2,1)S(1)}, u32[]{:S(2)}, u32[]{:S(2)}) async-start(bf16[128,4,256]{0,2,1:T(8,128)(2,1)} %bitcast), calls=%async_computation | async-start | bytes 524288 | tf_op jit(solution)/shard_map/all_to_all | solution.py:21
  23.0 35.0 %all-to-all-start.2 = ((bf16[128,4,256]{0,2,1:T(8,128)(2,1)}), bf16[128,4,256]{0,2,1:T(8,128)(2,1)S(1)}, u32[]{:S(2)}, u32[]{:S(2)}) async-start(bf16[128,4,256]{0,2,1:T(8,128)(2,1)} %bitcast.10), calls=%async_computation.2 | async-start | bytes 524288 | tf_op jit(solution)/shard_map/all_to_all | solution.py:20
  26.6 19.1 %collective-permute-start.1 = (bf16[512,512]{1,0:T(8,128)(2,1)S(1)}, bf16[512,512]{1,0:T(8,128)(2,1)S(1)}, u32[]{:S(2)}, u32[]{:S(2)}) collective-permute-start(bf16[512,512]{1,0:T(8,128)(2,1)S(1)} %pad_maximum_fusion), channel_id=1, source_target_pairs={{0,4},{4,8},{8,12},{1,5},{5,9},{9,13},{2,6},{6,10},{10,14},{3,7},{... | collective-permute-start | bytes 1572872 | tf_op jit(solution)/shard_map/ppermute | solution.py:15
  28.1 17.7 %collective-permute-start = (bf16[256,512]{1,0:T(8,128)(2,1)S(1)}, bf16[256,512]{1,0:T(8,128)(2,1)S(1)}, u32[]{:S(2)}, u32[]{:S(2)}) collective-permute-start(bf16[256,512]{1,0:T(8,128)(2,1)S(1)} %fusion.21), channel_id=1, source_target_pairs={{0,8},{4,12},{1,9},{5,13},{2,10},{6,14},{3,11},{7,15},{16,24},{20,... | collective-permute-start | bytes 786440 | tf_op jit(solution)/shard_map/ppermute | solution.py:15
  58.0 3.8 %copy-start.1 = (bf16[4,896,256]{1,2,0:T(8,128)(2,1)S(1)}, bf16[4,896,256]{1,2,0:T(8,128)(2,1)}, u32[]{:S(2)}) copy-start(bf16[4,896,256]{1,2,0:T(8,128)(2,1)} %copy.20) | copy-start | bytes 5505028
where the time goes:
time: 76.8 us; the launch traced here: 76.2 us
  waiting for transfers between devices  24.1 us (31%)
  local copies, waits for them, and re-layouts  18.9 us (25%)
  starting transfers between devices  14 us (18%)
  blocking collectives  12.3 us (16%)
  matrix products  4.02 us (5%)
  other arithmetic  2.02 us (3%)
  between operations  0.81 us (1%)
    ppermute x2, waiting for transfers between devices, shifted(): return lax.ppermute(value, axis, pairs)  16.3 us
    all_to_all x1, blocking collectives, local(): lax.all_to_all(gated, 'head', split_axis=0, concat_axis=1, tiled=True)  12.3 us
    slice x2, local copies, waits for them, and re-layouts, one_block(): picked[:, :, :width].reshape(4, listed * TILE, heads_here, HEAD_SIZE)  5.92 us
    unnamed x11, local copies, waits for them, and re-layouts  5.49 us
    all_to_all x1, waiting for transfers between devices, local(): lax.all_to_all(values, 'head', split_axis=1, concat_axis=0, tiled=True)  5.09 us
    all_to_all x1, starting transfers between devices, local(): lax.all_to_all(values, 'head', split_axis=1, concat_axis=0, tiled=True)  4.59 us
    slice x1, local copies, waits for them, and re-layouts, one_block(): picked[:, :, width:].reshape(4, listed * TILE, heads_here, HEAD_SIZE)  3.6 us
    all_to_all x1, starting transfers between devices, local(): lax.all_to_all(queries, 'head', split_axis=1, concat_axis=0, tiled=True)  3.41 us
  transfers between devices with their start and end apart: 5, of which 3 were waited for; matrix products, arithmetic and copies ran while one was open for 23% of the time, Pallas kernels for 0%

commit v1 on v0

--- a/solution.py
+++ b/solution.py
@@ -9,6 +9,22 @@
 FREQ = 256
 
 
+def pairwise_exchange(shard, axis, split, join):
+    ways, here = (lax.axis_size(axis), lax.axis_index(axis))
+    width = shard.shape[split] // ways
+    shape = list(shard.shape)
+    shape[split] = width
+    height = shape[join]
+    shape[join] = height * ways
+    full = jnp.zeros(shape, shard.dtype)
+    for mask in range(ways):
+        part = lax.dynamic_slice_in_dim(shard, (here ^ mask) * width, width, axis=split)
+        if mask:
+            part = lax.ppermute(part, axis, [(d, d ^ mask) for d in range(ways)])
+        full = lax.dynamic_update_slice_in_dim(full, part, (here ^ mask) * height, axis=join)
+    return full
+
+
 def shifted(value, axis, by):
     size = lax.axis_size(axis)
     pairs = [(i, i + by) for i in range(size) if 0 <= i + by < size]
@@ -18,7 +34,7 @@
 def local(queries, keys, values, tile_offsets, timesteps, time_weight):
     query_heads, key_heads, value_heads = (
         lax.all_to_all(queries, "head", split_axis=1, concat_axis=0, tiled=True),
-        lax.all_to_all(keys, "head", split_axis=1, concat_axis=0, tiled=True),
+        pairwise_exchange(keys, "head", 1, 0),
         lax.all_to_all(values, "head", split_axis=1, concat_axis=0, tiled=True),
     )
     span_rows = query_heads.shape[0]

time: 76.8 us -> 71.3 us (0.928)
  waiting for transfers between devices: 24.1 us -> 18.6 us
  local copies, waits for them, and re-layouts: 18.9 us -> 17.9 us
  starting transfers between devices: 14 us -> 15 us
    all_to_all x1, waiting for transfers between devices: 5.09 us -> 0.01 us  [local(): lax.all_to_all(values, 'head', split_axis=1, concat_axis=0, tiled=True)]
    ppermute x0 -> x3, starting transfers between devices: none -> 3.69 us  [pairwise_exchange(): part = lax.ppermute(part, axis, [(d, d ^ mask) for d in range(ways)])]
    all_to_all x1 -> x0, starting transfers between devices: 3.4 us -> none  [local(): lax.all_to_all(keys, 'head', split_axis=1, concat_axis=0, tiled=True)]
    ppermute x0 -> x3, waiting for transfers between devices: none -> 3.34 us  [pairwise_exchange(): part = lax.ppermute(part, axis, [(d, d ^ mask) for d in range(ways)])]
    all_to_all x1 -> x0, waiting for transfers between devices: 2.69 us -> none  [local(): lax.all_to_all(keys, 'head', split_axis=1, concat_axis=0, tiled=True)]
    unnamed x11 -> x10, local copies, waits for them, and re-layouts: 5.49 us -> 3.77 us
    ppermute x2, waiting for transfers between devices: 16.3 us -> 15.3 us  [shifted(): return lax.ppermute(value, axis, pairs)]
    dynamic_slice x0 -> x1, local copies, waits for them, and re-layouts: none -> 0.97 us  [pairwise_exchange(): lax.dynamic_slice_in_dim(shard, (here ^ mask) * width, width, axis=split)]
  transfers between devices with their start and end apart: 5 -> 7, of which waited for: 3 -> 3; matrix products, arithmetic and copies ran while one was open for 23% -> 23% of each run, Pallas kernels for 0% -> 0%
where the time goes in v1:
time: 71.3 us; the launch traced here: 70.7 us
  waiting for transfers between devices  18.6 us (26%)
  local copies, waits for them, and re-layouts  17.9 us (25%)
  starting transfers between devices  15 us (21%)
  blocking collectives  12.3 us (17%)
  matrix products  4.02 us (6%)
  other arithmetic  2.02 us (3%)
  between operations  0.81 us (1%)
    ppermute x2, waiting for transfers between devices, shifted(): return lax.ppermute(value, axis, pairs)  15.3 us
    all_to_all x1, blocking collectives, local(): lax.all_to_all(gated, 'head', split_axis=0, concat_axis=1, tiled=True)  12.3 us
    slice x2, local copies, waits for them, and re-layouts, one_block(): picked[:, :, :width].reshape(4, listed * TILE, heads_here, HEAD_SIZE)  5.89 us
    all_to_all x1, starting transfers between devices, local(): lax.all_to_all(values, 'head', split_axis=1, concat_axis=0, tiled=True)  4.59 us
    all_to_all x1, starting transfers between devices, local(): lax.all_to_all(queries, 'head', split_axis=1, concat_axis=0, tiled=True)  4.1 us
    unnamed x10, local copies, waits for them, and re-layouts  3.77 us
    ppermute x3, starting transfers between devices, pairwise_exchange(): part = lax.ppermute(part, axis, [(d, d ^ mask) for d in range(ways)])  3.69 us
    slice x1, local copies, waits for them, and re-layouts, one_block(): picked[:, :, width:].reshape(4, listed * TILE, heads_here, HEAD_SIZE)  3.56 us
  transfers between devices with their start and end apart: 7, of which 3 were waited for; matrix products, arithmetic and copies ran while one was open for 23% of the time, Pallas kernels for 0%

profile of v1, /device:TPU:7, one launch (start us, length us, event | category | flops | bytes accessed | tf_op | source)
XLA Modules:
  0.0 70.7 jit_solution(9458985991420652630)
XLA Ops:
  0.0 0.0 copy-start
  0.0 0.0 copy-start.2
  0.0 1.8 %copy.16 = bf16[128,1024]{0,1:T(8,128)(2,1)} copy(bf16[128,1024]{1,0:T(8,128)(2,1)} %param.8) | data formatting | bytes 524288 | tf_op args[2]
  1.8 4.6 %all-to-all-start = ((bf16[128,4,256]{0,2,1:T(8,128)(2,1)}), bf16[128,4,256]{0,2,1:T(8,128)(2,1)S(1)}, u32[]{:S(2)}, u32[]{:S(2)}) async-start(bf16[128,4,256]{0,2,1:T(8,128)(2,1)} %bitcast), calls=%async_computation | async-start | bytes 524288 | tf_op jit(solution)/shard_map/all_to_all | solution.py:38
  6.4 1.0 %constant_dynamic-slice_fusion = (bf16[128,256]{1,0:T(8,128)(2,1)S(1)}, bf16[128,256]{1,0:T(8,128)(2,1)S(1)}, bf16[512,256]{1,0:T(8,128)(2,1)S(1)}, bf16[128,256]{1,0:T(8,128)(2,1)S(1)}) fusion(bf16[128,1024]{1,0:T(8,128)(2,1)} %param.7, s32[]{:T(128)S(6)} %select_n.46, s32[]{:T(128)S(6)} %select_n.42, bf16[512,256]{1,0:T(8,128)(2,1)S(1)} %broadcast_in_dim.41, ...), kind=kLoop, calls=%fused_computation.32 | loop fusion | bytes 524308 | tf_op jit(solution)/shard_map/dynamic_slice | solution.py:21
  7.4 1.5 %collective-permute-start = (bf16[128,256]{1,0:T(8,128)(2,1)S(1)}, bf16[128,256]{1,0:T(8,128)(2,1)S(1)}, u32[]{:S(2)}, u32[]{:S(2)}) collective-permute-start(bf16[128,256]{1,0:T(8,128)(2,1)S(1)} %get-tuple-element.20), channel_id=1, source_target_pairs={{0,1},{1,0},{2,3},{3,2},{4,5},{5,4},{6,7},{7,6},{8,9},{9,8},{10,11... | collective-permute-start | bytes 196616 | tf_op jit(solution)/shard_map/ppermute | solution.py:23
  8.9 2.1 %collective-permute-start.1 = (bf16[128,256]{1,0:T(8,128)(2,1)S(1)}, bf16[128,256]{1,0:T(8,128)(2,1)S(1)}, u32[]{:S(2)}, u32[]{:S(2)}) collective-permute-start(bf16[128,256]{1,0:T(8,128)(2,1)S(1)} %get-tuple-element.30), channel_id=1, source_target_pairs={{0,2},{1,3},{2,0},{3,1},{4,6},{5,7},{6,4},{7,5},{8,10},{9,11},{10,... | collective-permute-start | bytes 196616 | tf_op jit(solution)/shard_map/ppermute | solution.py:23
  11.0 0.1 collective-permute-start.2
  11.8 0.1 fusion.27
  11.8 0.7 add_compare_fusion
  12.5 0.0 copy-done
  12.5 0.1 fusion.22
  12.7 0.1 broadcast_bitcast_fusion
  12.7 1.9 %copy.20 = bf16[128,1024]{0,1:T(8,128)(2,1)} copy(bf16[128,1024]{1,0:T(8,128)(2,1)} %param.6) | data formatting | bytes 524288 | tf_op args[0]
  14.6 0.0 collective-permute-done
  14.6 2.6 %collective-permute-done.1 = bf16[128,256]{1,0:T(8,128)(2,1)S(1)} collective-permute-done((bf16[128,256]{1,0:T(8,128)(2,1)S(1)}, bf16[128,256]{1,0:T(8,128)(2,1)S(1)}, u32[]{:S(2)}, u32[]{:S(2)}) %collective-permute-start.1) | collective-permute-done | bytes 65568 | tf_op jit(solution)/shard_map/ppermute | solution.py:23
  17.2 0.8 %collective-permute-done.2 = bf16[128,256]{1,0:T(8,128)(2,1)S(1)} collective-permute-done((bf16[128,256]{1,0:T(8,128)(2,1)S(1)}, bf16[128,256]{1,0:T(8,128)(2,1)S(1)}, u32[]{:S(2)}, u32[]{:S(2)}) %collective-permute-start.2) | collective-permute-done | bytes 65568 | tf_op jit(solution)/shard_map/ppermute | solution.py:23
  18.0 0.0 all-to-all-done
  18.0 4.1 %all-to-all-start.1 = ((bf16[128,4,256]{0,2,1:T(8,128)(2,1)}), bf16[128,4,256]{0,2,1:T(8,128)(2,1)S(1)}, u32[]{:S(2)}, u32[]{:S(2)}) async-start(bf16[128,4,256]{0,2,1:T(8,128)(2,1)} %bitcast.7), calls=%async_computation.1 | async-start | bytes 524288 | tf_op jit(solution)/shard_map/all_to_all | solution.py:36
  22.1 0.1 copy.17
  22.3 1.3 %collective-permute-start.4 = (bf16[512,512]{1,0:T(8,128)(2,1)S(1)}, bf16[512,512]{1,0:T(8,128)(2,1)S(1)}, u32[]{:S(2)}, u32[]{:S(2)}) collective-permute-start(bf16[512,512]{1,0:T(8,128)(2,1)S(1)} %pad_maximum_fusion), channel_id=1, source_target_pairs={{0,4},{4,8},{8,12},{1,5},{5,9},{9,13},{2,6},{6,10},{10,14},{3,7},{... | collective-permute-start | bytes 1572872 | tf_op jit(solution)/shard_map/ppermute | solution.py:31
  23.6 0.0 copy-done.2
  23.6 0.1 reshape.94
  23.7 1.3 %collective-permute-start.3 = (bf16[256,512]{1,0:T(8,128)(2,1)S(1)}, bf16[256,512]{1,0:T(8,128)(2,1)S(1)}, u32[]{:S(2)}, u32[]{:S(2)}) collective-permute-start(bf16[256,512]{1,0:T(8,128)(2,1)S(1)} %fusion.21), channel_id=1, source_target_pairs={{0,8},{4,12},{1,9},{5,13},{2,10},{6,14},{3,11},{7,15},{16,24},{20,... | collective-permute-start | bytes 786440 | tf_op jit(solution)/shard_map/ppermute | solution.py:31
  25.0 15.3 %collective-permute-done.3 = bf16[256,512]{1,0:T(8,128)(2,1)S(1)} collective-permute-done((bf16[256,512]{1,0:T(8,128)(2,1)S(1)}, bf16[256,512]{1,0:T(8,128)(2,1)S(1)}, u32[]{:S(2)}, u32[]{:S(2)}) %collective-permute-start.3) | collective-permute-done | bytes 262176 | tf_op jit(solution)/shard_map/ppermute | solution.py:31
  40.3 0.0 collective-permute-done.4
  40.3 0.1 maximum_maximum_fusion
  40.4 2.6 %gather_fusion = bf16[28,128,512]{2,1,0:T(8,128)(2,1)} fusion(bf16[10,128,512]{2,1,0:T(8,128)(2,1)S(1)} %bitcast.70, s32[1024]{0:T(1024)S(1)} %pad_clamp_fusion), kind=kCustom, calls=%fused_computation | custom fusion | bytes 7340144 | tf_op jit(solution)/shard_map/while/body/eval_jaxpr/gather | solution.py:68
  43.0 3.6 %fusion.32 = (bf16[4,896,256]{2,1,0:T(8,128)(2,1)S(1)}, bf16[4,896,256]{2,1,0:T(8,128)(2,1)}) fusion(bf16[4,896,512]{2,1,0:T(8,128)(2,1)} %bitcast.71), kind=kLoop, calls=%fused_computation.47 | loop fusion | bytes 7340032 | tf_op jit(solution)/shard_map/while/body/eval_jaxpr/slice | solution.py:69
  46.6 3.6 %copy.18 = bf16[4,896,256]{1,2,0:T(8,128)(2,1)} copy(bf16[4,896,256]{2,1,0:T(8,128)(2,1)} %get-tuple-element.18) | data formatting | bytes 3670016 | tf_op jit(solution)/shard_map/while/body/eval_jaxpr/slice | solution.py:70
  50.2 2.3 %copy.19 = bf16[4,896,256]{1,2,0:T(8,128)(2,1)} copy(bf16[4,896,256]{2,1,0:T(8,128)(2,1)S(1)} %get-tuple-element.17) | data formatting | bytes 3670016 | tf_op jit(solution)/shard_map/while/body/eval_jaxpr/slice | solution.py:69
  52.5 0.0 all-to-all-done.1
  52.5 0.0 copy-start.1
  52.5 2.6 %bitcast_reduce_fusion = (f32[4,2,128]{2,1,0:T(2,128)S(1)}, f32[4,2,896,128]{3,2,1,0:T(8,128)S(1)}) fusion(pred[4,896]{1,0:T(4,128)(4,1)S(1)} %bitcast.81, bf16[4,896,2,128]{1,3,2,0:T(8,128)(2,1)} %bitcast.72, bf16[4,128,2,128]{1,3,2,0:T(8,128)(2,1)S(1)} %bitcast.79), kind=kOutput, calls=%fused_computation.2 | convolution fusion | flops 237632512 | bytes 5774848 | tf_op jit(solution)/shard_map/while/body/eval_jaxpr/qthd,qkhd->qhtk/dot_general | solution.py:72
  55.1 1.1 %fusion.1 = f32[4,2,128]{2,1,0:T(2,128)S(1)} fusion(f32[4,2,896,128]{3,2,1,0:T(8,128)S(1)} %get-tuple-element.33, f32[4,2,128]{2,1,0:T(2,128)S(1)} %get-tuple-element.32, pred[4,896]{1,0:T(4,128)(4,1)S(1)} %bitcast.82), kind=kLoop, calls=%fused_computation.5 | loop fusion | flops 3668992 | bytes 3681792 | tf_op jit(solution)/shard_map/while/body/eval_jaxpr/reduce_sum | solution.py:79
  56.2 0.0 copy-done.1
  56.3 1.3 %fusion.18 = bf16[4,128,2,128]{1,3,2,0:T(8,128)(2,1)S(1)} fusion(bf16[4,896,2,128]{1,3,2,0:T(8,128)(2,1)S(1)} %bitcast.76, f32[4,2,896,128]{3,2,1,0:T(8,128)S(1)} %get-tuple-element.33, f32[4,2,128]{2,1,0:T(2,128)S(1)} %get-tuple-element.32, pred[4,896]{1,0:T(4,128)(4,1)S(1)} %bitcast.83, f32[2,128]{1,0:T(2,128)S(1)} %broadcast_add_fusion, ...), kind=kOutput, calls=%fused_computation.16 | convolution fusion | flops 238944256 | bytes 5779968 | tf_op jit(solution)/shard_map/while/body/eval_jaxpr/qhtk,qkhd->qthd/dot_general | solution.py:81
  57.5 12.3 %all_to_all.54 = bf16[4,128,256]{1,2,0:T(8,128)(2,1)S(1)} all-to-all(bf16[4,128,256]{1,2,0:T(8,128)(2,1)S(1)} %bitcast.80), channel_id=1, replica_groups=mesh['groups'=2,'span'=4,'head'=4] {'head'}, dimensions={0} | all-to-all | bytes 524288 | tf_op jit(solution)/shard_map/all_to_all | solution.py:89
  69.9 0.8 %copy.30 = bf16[128,1024]{1,0:T(8,128)(2,1)} copy(bf16[128,1024]{0,1:T(8,128)(2,1)S(1)} %bitcast.78) | data formatting | bytes 524288 | tf_op jit(solution)/shard_map/all_to_all | solution.py:89
  (10 shorter events, 0.1 us)
Async XLA Ops:
  0.0 12.5 %copy-start = (bf16[256,256]{1,0:T(8,128)(2,1)S(1)}, bf16[256,256]{1,0:T(8,128)(2,1)}, u32[]{:S(2)}) copy-start(bf16[256,256]{1,0:T(8,128)(2,1)} %param.11) | copy-start | bytes 393220
  0.0 23.6 %copy-start.2 = (s32[4,7]{1,0:T(4,128)S(1)}, s32[4,7]{1,0:T(4,128)}, u32[]{:S(2)}) copy-start(s32[4,7]{1,0:T(4,128)} %param.9) | copy-start | bytes 340
  1.8 16.1 %all-to-all-start = ((bf16[128,4,256]{0,2,1:T(8,128)(2,1)}), bf16[128,4,256]{0,2,1:T(8,128)(2,1)S(1)}, u32[]{:S(2)}, u32[]{:S(2)}) async-start(bf16[128,4,256]{0,2,1:T(8,128)(2,1)} %bitcast), calls=%async_computation | async-start | bytes 524288 | tf_op jit(solution)/shard_map/all_to_all | solution.py:38
  7.4 7.2 %collective-permute-start = (bf16[128,256]{1,0:T(8,128)(2,1)S(1)}, bf16[128,256]{1,0:T(8,128)(2,1)S(1)}, u32[]{:S(2)}, u32[]{:S(2)}) collective-permute-start(bf16[128,256]{1,0:T(8,128)(2,1)S(1)} %get-tuple-element.20), channel_id=1, source_target_pairs={{0,1},{1,0},{2,3},{3,2},{4,5},{5,4},{6,7},{7,6},{8,9},{9,8},{10,11... | collective-permute-start | bytes 196616 | tf_op jit(solution)/shard_map/ppermute | solution.py:23
  8.9 8.2 %collective-permute-start.1 = (bf16[128,256]{1,0:T(8,128)(2,1)S(1)}, bf16[128,256]{1,0:T(8,128)(2,1)S(1)}, u32[]{:S(2)}, u32[]{:S(2)}) collective-permute-start(bf16[128,256]{1,0:T(8,128)(2,1)S(1)} %get-tuple-element.30), channel_id=1, source_target_pairs={{0,2},{1,3},{2,0},{3,1},{4,6},{5,7},{6,4},{7,5},{8,10},{9,11},{10,... | collective-permute-start | bytes 196616 | tf_op jit(solution)/shard_map/ppermute | solution.py:23
  11.0 6.9 %collective-permute-start.2 = (bf16[128,256]{1,0:T(8,128)(2,1)S(1)}, bf16[128,256]{1,0:T(8,128)(2,1)S(1)}, u32[]{:S(2)}, u32[]{:S(2)}) collective-permute-start(bf16[128,256]{1,0:T(8,128)(2,1)S(1)} %get-tuple-element.19), channel_id=1, source_target_pairs={{0,3},{1,2},{2,1},{3,0},{4,7},{5,6},{6,5},{7,4},{8,11},{9,10},{10,... | collective-permute-start | bytes 196616 | tf_op jit(solution)/shard_map/ppermute | solution.py:23
  18.0 34.5 %all-to-all-start.1 = ((bf16[128,4,256]{0,2,1:T(8,128)(2,1)}), bf16[128,4,256]{0,2,1:T(8,128)(2,1)S(1)}, u32[]{:S(2)}, u32[]{:S(2)}) async-start(bf16[128,4,256]{0,2,1:T(8,128)(2,1)} %bitcast.7), calls=%async_computation.1 | async-start | bytes 524288 | tf_op jit(solution)/shard_map/all_to_all | solution.py:36
  22.3 18.1 %collective-permute-start.4 = (bf16[512,512]{1,0:T(8,128)(2,1)S(1)}, bf16[512,512]{1,0:T(8,128)(2,1)S(1)}, u32[]{:S(2)}, u32[]{:S(2)}) collective-permute-start(bf16[512,512]{1,0:T(8,128)(2,1)S(1)} %pad_maximum_fusion), channel_id=1, source_target_pairs={{0,4},{4,8},{8,12},{1,5},{5,9},{9,13},{2,6},{6,10},{10,14},{3,7},{... | collective-permute-start | bytes 1572872 | tf_op jit(solution)/shard_map/ppermute | solution.py:31
  23.7 16.6 %collective-permute-start.3 = (bf16[256,512]{1,0:T(8,128)(2,1)S(1)}, bf16[256,512]{1,0:T(8,128)(2,1)S(1)}, u32[]{:S(2)}, u32[]{:S(2)}) collective-permute-start(bf16[256,512]{1,0:T(8,128)(2,1)S(1)} %fusion.21), channel_id=1, source_target_pairs={{0,8},{4,12},{1,9},{5,13},{2,10},{6,14},{3,11},{7,15},{16,24},{20,... | collective-permute-start | bytes 786440 | tf_op jit(solution)/shard_map/ppermute | solution.py:31
  52.5 3.8 %copy-start.1 = (bf16[4,896,256]{1,2,0:T(8,128)(2,1)S(1)}, bf16[4,896,256]{1,2,0:T(8,128)(2,1)}, u32[]{:S(2)}) copy-start(bf16[4,896,256]{1,2,0:T(8,128)(2,1)} %copy.18) | copy-start | bytes 5505028
